TPU v7x, 256 devices: a whole 4x4x8 slice. The times are simulated.
256 devices in a mesh: gx: 16 (over z_lo, x), gy: 16 (over y, z_hi, core).
Axes of the slice: x: 4, y: 4, z: 8 (z_hi: 2, z_lo: 4; z = z_hi * 4 + z_lo), core: 2. Of those that a mesh axis runs over, the one named last changes fastest.
Arguments:
- features: float32 [16, 128, 256, 128], P(None, 'gx', 'gy'), may hold values from -6 to 6
- conv_weight: float32 [27, 16, 16], replicated, may hold values from -0.3125 to 0.3125
- mix_weight: float32 [2, 16, 16, 16, 432], P(None, None, None, 'gy', 'gx'), may hold values from -1 to 1
Outputs:
- layer_out: float32 [16, 128, 256, 128], P(None, 'gx', 'gy')
All inputs are finite; a program needn't handle non-finite values.
Results may differ from a plain program's by a relative error of at most 0.0001.
Values sent between devices are 32-bit elements; how exact they have to be, the bound alone decides.
A program may use at most 128 MiB of HBM per device.

v0:
```python
import math
import jax
import jax.numpy as jnp
from jax import lax
from jax.sharding import PartitionSpec as P

KX = 24
KY = 24
KZ = 12
PRECISE = lax.Precision.HIGHEST


def padded_2(array, sides, width):
    for axis, dim in sides:
        size, length = (lax.axis_size(axis), array.shape[dim])
        up = [(i, (i + 1) % size) for i in range(size)]
        down = [(j, i) for i, j in up]
        last = lax.slice_in_dim(array, length - width, length, axis=dim)
        initial = lax.slice_in_dim(array, 0, width, axis=dim)
        before = lax.ppermute(last, axis, up)
        after = lax.ppermute(initial, axis, down)
        array = jnp.concatenate([before, array, after], axis=dim)
    return array


def angle_tables(positions, frequencies, length):
    product = positions[:, None] * frequencies[None, :] % length
    angles = product.astype(jnp.float32) * (2.0 * math.pi / length)
    return (jnp.cos(angles), jnp.sin(angles))


def kept_frequencies(amount, length):
    index = jnp.arange(amount, dtype=jnp.int32)
    return jnp.where(index < amount // 2, index, length - amount + index)


def forward_x(part_real, part_imag, cos_x, sin_x):
    out_real = jnp.einsum("cxm,xp->cpm", part_real, cos_x, precision=PRECISE) + jnp.einsum(
        "cxm,xp->cpm", part_imag, sin_x, precision=PRECISE
    )
    out_imag = jnp.einsum("cxm,xp->cpm", part_imag, cos_x, precision=PRECISE) - jnp.einsum(
        "cxm,xp->cpm", part_real, sin_x, precision=PRECISE
    )
    return (out_real, out_imag)


def inverse_x(part_real, part_imag, cos_x, sin_x):
    out_real = jnp.einsum("cpm,xp->cxm", part_real, cos_x, precision=PRECISE) - jnp.einsum(
        "cpm,xp->cxm", part_imag, sin_x, precision=PRECISE
    )
    out_imag = jnp.einsum("cpm,xp->cxm", part_imag, cos_x, precision=PRECISE) + jnp.einsum(
        "cpm,xp->cxm", part_real, sin_x, precision=PRECISE
    )
    return (out_real, out_imag)


def shards(features, conv_weight, mix_weight):
    channels, cells_x, cells_y, length_z = features.shape
    count_gx = lax.axis_size("gx")
    count_gy = lax.axis_size("gy")
    length_x = cells_x * count_gx
    length_y = cells_y * count_gy
    block_yz = KY * KZ // count_gy
    padded = padded_2(features, (("gx", 1), ("gy", 2)), 1)
    wrapped = jnp.concatenate([padded[..., -1:], padded, padded[..., :1]], axis=3)
    kernel = conv_weight.reshape(3, 3, 3, channels, channels).transpose(3, 4, 0, 1, 2)
    conv_sum = lax.conv_general_dilated(
        wrapped[None],
        kernel,
        (1, 1, 1),
        "VALID",
        dimension_numbers=("NCDHW", "OIDHW", "NCDHW"),
        precision=PRECISE,
    )[0]
    cos_z, sin_z = angle_tables(
        jnp.arange(length_z, dtype=jnp.int32), jnp.arange(KZ, dtype=jnp.int32), length_z
    )
    y_places = lax.axis_index("gy") * cells_y + jnp.arange(cells_y, dtype=jnp.int32)
    x_places = lax.axis_index("gx") * cells_x + jnp.arange(cells_x, dtype=jnp.int32)
    cos_y, sin_y = angle_tables(y_places, kept_frequencies(KY, length_y), length_y)
    cos_x, sin_x = angle_tables(x_places, kept_frequencies(KX, length_x), length_x)
    table_z = jnp.concatenate([cos_z, -sin_z], axis=1)
    along_z = jnp.dot(features, table_z, precision=PRECISE)
    z_real = along_z[..., :KZ]
    z_imag = along_z[..., KZ:]
    y_real = jnp.einsum("cxyk,yq->cxqk", z_real, cos_y, precision=PRECISE) + jnp.einsum(
        "cxyk,yq->cxqk", z_imag, sin_y, precision=PRECISE
    )
    y_imag = jnp.einsum("cxyk,yq->cxqk", z_imag, cos_y, precision=PRECISE) - jnp.einsum(
        "cxyk,yq->cxqk", z_real, sin_y, precision=PRECISE
    )
    partial_value = jnp.stack([y_real, y_imag], axis=2).reshape(channels, cells_x, 2, KY * KZ)
    y_share = lax.psum_scatter(partial_value, "gy", scatter_dimension=3, tiled=True)
    x_real, x_imag = forward_x(y_share[:, :, 0], y_share[:, :, 1], cos_x, sin_x)
    x_partial = jnp.stack([x_real, x_imag], axis=1).reshape(channels, 2, KX * block_yz)
    owned_modes = lax.psum_scatter(x_partial, "gx", scatter_dimension=2, tiled=True)
    forward_scale = 1.0 / math.sqrt(length_x * length_y * length_z)
    owned_modes = owned_modes * forward_scale
    coef_real = owned_modes[:, 0]
    coef_imag = owned_modes[:, 1]
    weight_real = mix_weight[0, :, :, 0, :]
    weight_imag = mix_weight[1, :, :, 0, :]
    mixed_real = jnp.einsum("oim,im->om", weight_real, coef_real, precision=PRECISE) - jnp.einsum(
        "oim,im->om", weight_imag, coef_imag, precision=PRECISE
    )
    mixed_imag = jnp.einsum("oim,im->om", weight_real, coef_imag, precision=PRECISE) + jnp.einsum(
        "oim,im->om", weight_imag, coef_real, precision=PRECISE
    )
    mixed_modes = jnp.stack([mixed_real, mixed_imag], axis=1)
    row_modes = lax.all_gather(mixed_modes, "gx", axis=2, tiled=True).reshape(
        channels, 2, KX, block_yz
    )
    back_real, back_imag = inverse_x(row_modes[:, 0], row_modes[:, 1], cos_x, sin_x)
    x_inverse = jnp.stack([back_real, back_imag], axis=2)
    gathered = lax.all_gather(x_inverse, "gy", axis=3, tiled=True)
    back_real = gathered[:, :, 0].reshape(channels, cells_x, KY, KZ)
    back_imag = gathered[:, :, 1].reshape(channels, cells_x, KY, KZ)
    plane_real = jnp.einsum("cxqk,yq->cxyk", back_real, cos_y, precision=PRECISE) - jnp.einsum(
        "cxqk,yq->cxyk", back_imag, sin_y, precision=PRECISE
    )
    plane_imag = jnp.einsum("cxqk,yq->cxyk", back_imag, cos_y, precision=PRECISE) + jnp.einsum(
        "cxqk,yq->cxyk", back_real, sin_y, precision=PRECISE
    )
    table_back = jnp.concatenate([cos_z.T, -sin_z.T], axis=0)
    inverse_scale = 1.0 / math.sqrt(KX * KY * KZ)
    spectral = (
        jnp.dot(jnp.concatenate([plane_real, plane_imag], axis=3), table_back, precision=PRECISE)
        * inverse_scale
    )
    return jax.nn.gelu(conv_sum + spectral, approximate=False)


def solution(mesh):
    in_specs = (P(None, "gx", "gy", None), P(), P(None, None, None, "gy", "gx"))
    out_specs = P(None, "gx", "gy", None)
    return jax.shard_map(shards, mesh=mesh, in_specs=in_specs, out_specs=out_specs, check_vma=False)
```

profile of v0, /device:TPU:7, one launch (start us, length us, event | category | flops | bytes accessed | tf_op | source)
XLA Modules:
  0.0 493.7 jit_solution(6698932705271622397)
XLA Ops:
  6.6 2.2 convolution_bitcast_fusion
  10.1 2.1 copy.51
  14.9 1.8 fusion.13
  16.7 2.0 copy.53
  22.3 1.6 collective-permute-start
  27.6 2.3 collective-permute-done.1
  30.0 8.1 %collective-permute-start.2 = (f32[16,10,1,128]{3,0,2,1:T(8,128)S(1)}, f32[16,10,1,128]{3,0,2,1:T(8,128)S(1)}, u32[]{:S(2)}, u32[]{:S(2)}) collective-permute-start(f32[16,10,1,128]{3,0,2,1:T(8,128)S(1)} %get-tuple-element.15), channel_id=1, source_target_pairs={{0,1},{1,2},{2,3},{3,4},{4,5},{5,6},{6,7},{7,8},{8,9},{9,10},{10,1... | collective-permute-start | bytes 245768 | tf_op jit(solution)/shard_map/ppermute | solution.py:20
  39.5 7.2 %collective-permute-done.3 = f32[16,10,1,128]{3,0,2,1:T(8,128)S(1)} collective-permute-done((f32[16,10,1,128]{3,0,2,1:T(8,128)S(1)}, f32[16,10,1,128]{3,0,2,1:T(8,128)S(1)}, u32[]{:S(2)}, u32[]{:S(2)}) %collective-permute-start.3) | collective-permute-done | bytes 81952 | tf_op jit(solution)/shard_map/ppermute | solution.py:21
  48.9 6.5 %reshape.44 = f32[16,10,18,1,8,17]{5,4,0,2,1,3:T(8,128)} reshape(f32[16,10,18,1,136]{4,0,2,1,3:T(8,128)S(1)} %pad) | data formatting | bytes 3133440 | tf_op jit(solution)/shard_map/conv_general_dilated | solution.py:67
  55.4 15.0 %copy.47 = f32[16,10,18,1,8,17]{0,4,5,2,1,3:T(8,128)} copy(f32[16,10,18,1,8,17]{5,4,0,2,1,3:T(8,128)} %reshape.44) | data formatting | bytes 3133440 | tf_op jit(solution)/shard_map/conv_general_dilated | solution.py:67
  70.4 1.5 slice.80
  71.9 5.3 %fusion.197 = f32[16,10,18,8,19]{0,3,4,2,1:T(8,128)S(1)} fusion(f32[16,10,18,1,7,2]{0,4,5,2,1,3:T(8,128)S(1)} %slice.80, f32[16,10,18,1,8,17]{0,4,5,2,1,3:T(8,128)} %copy.47), kind=kLoop, calls=%fused_computation.1.clone.clone.clone.clone.1 | loop fusion | flops 1313280 | bytes 3479040 | tf_op jit(solution)/shard_map/conv_general_dilated | solution.py:67
  77.2 193.4 %broadcast_select_fusion = f32[8,16,8,17,16]{4,2,3,1,0:T(8,128)} fusion(pred[8,17]{0,1:T(8,128)(4,1)S(1)} %copy-done.7, f32[3,3,3,16,16]{4,3,2,1,0:T(8,128)S(1)} %bitcast.181, f32[16,10,18,8,19]{0,3,4,2,1:T(8,128)S(1)} %fusion.197), kind=kOutput, calls=%fused_computation.8 | convolution fusion | flops 1444167680 | bytes 2892936 | tf_op jit(solution)/shard_map/conv_general_dilated | solution.py:67
  270.7 12.7 %copy.98 = f32[8,16,8,17,16]{3,2,1,0,4:T(8,128)} copy(f32[8,16,8,17,16]{4,2,3,1,0:T(8,128)} %broadcast_select_fusion) | data formatting | bytes 2228224 | tf_op jit(solution)/shard_map/conv_general_dilated | solution.py:67
  283.4 7.0 %reshape.68 = f32[8,16,1,136,16]{3,1,0,4,2:T(8,128)} reshape(f32[8,16,8,17,16]{3,2,1,0,4:T(8,128)} %copy.98) | data formatting | bytes 2228224 | tf_op jit(solution)/shard_map/conv_general_dilated | solution.py:67
  291.8 1.4 fusion.15
  293.3 1.4 fusion.39
  296.3 57.2 %all-reduce.1 = f32[16,2,432]{2,0,1:T(8,128)S(1)} all-reduce(f32[16,2,432]{2,0,1:T(8,128)S(1)} %pad_maximum_fusion.3), channel_id=3, replica_groups=mesh['gx'=16,'gy'=16] {'gx'}, use_global_device_ids=true, to_apply=%region_1.2.clone | all-reduce | flops 13824 | bytes 110592
  353.8 38.1 %all_gather.6 = f32[16,2,432]{0,1,2:T(2,128)S(1)} all-gather(f32[16,2,27]{0,1,2:T(2,128)S(1)} %copy.57), channel_id=1, replica_groups=mesh['gx'=16,'gy'=16] {'gx'}, dimensions={2}, use_global_device_ids=true | all-gather | bytes 58752 | tf_op jit(solution)/shard_map/all_gather | solution.py:110
  394.2 76.2 %all_gather.7 = f32[16,8,2,288]{0,1,2,3:T(8,128)S(1)} all-gather(f32[16,8,2,18]{0,1,2,3:T(8,128)S(1)} %copy.59), channel_id=1, replica_groups=mesh['gx'=16,'gy'=16] {'gy'}, dimensions={3}, use_global_device_ids=true | all-gather | bytes 313344 | tf_op jit(solution)/shard_map/all_gather | solution.py:115
  471.5 1.7 copy.93
  473.2 2.2 fusion.59
  475.4 2.9 copy.94
  482.3 4.2 fusion.19
  (78 shorter events, 24.2 us)
Async XLA Ops:
  6.5 283.9 %all-reduce.4.cloned.1.call-start = ((), (), s32[]{:S(2)}) async-start(), calls=%async_computation | async-start | bytes 786432
  20.8 1.3 copy-start
  21.3 2.7 copy-start.3
  21.3 2.8 copy-start.6
  21.3 3.4 copy-start.5
  21.4 4.0 copy-start.4
  22.3 4.7 collective-permute-start
  23.9 6.0 %collective-permute-start.1 = (f32[16,1,16,128]{3,0,2,1:T(8,128)S(1)}, f32[16,1,16,128]{3,0,2,1:T(8,128)S(1)}, u32[]{:S(2)}, u32[]{:S(2)}) collective-permute-start(f32[16,1,16,128]{3,0,2,1:T(8,128)S(1)} %copy.121), channel_id=1, source_target_pairs={{16,0},{32,16},{48,32},{64,48},{80,64},{96,80},{112,96},{128,112},... | collective-permute-start | bytes 393224 | tf_op jit(solution)/shard_map/ppermute | solution.py:21
  30.0 9.6 %collective-permute-start.2 = (f32[16,10,1,128]{3,0,2,1:T(8,128)S(1)}, f32[16,10,1,128]{3,0,2,1:T(8,128)S(1)}, u32[]{:S(2)}, u32[]{:S(2)}) collective-permute-start(f32[16,10,1,128]{3,0,2,1:T(8,128)S(1)} %get-tuple-element.15), channel_id=1, source_target_pairs={{0,1},{1,2},{2,3},{3,4},{4,5},{5,6},{6,7},{7,8},{8,9},{9,10},{10,1... | collective-permute-start | bytes 245768 | tf_op jit(solution)/shard_map/ppermute | solution.py:20
  38.1 8.7 %collective-permute-start.3 = (f32[16,10,1,128]{3,0,2,1:T(8,128)S(1)}, f32[16,10,1,128]{3,0,2,1:T(8,128)S(1)}, u32[]{:S(2)}, u32[]{:S(2)}) collective-permute-start(f32[16,10,1,128]{3,0,2,1:T(8,128)S(1)} %get-tuple-element.16), channel_id=1, source_target_pairs={{1,0},{2,1},{3,2},{4,3},{5,4},{6,5},{7,6},{8,7},{9,8},{10,9},{11,1... | collective-permute-start | bytes 245768 | tf_op jit(solution)/shard_map/ppermute | solution.py:21
  71.9 5.3 %copy-start.7 = (pred[8,17]{0,1:T(8,128)(4,1)S(1)}, pred[8,17]{0,1:T(8,128)(4,1)}, u32[]{:S(2)}) copy-start(pred[8,17]{0,1:T(8,128)(4,1)} %constant.131) | copy-start | bytes 412
  478.3 1.2 copy-start.1
  480.7 1.6 copy-start.2
Sparse Core Ops, SparseCore 0:
  22.3 182.2 all-reduce.3
where the time goes:
time: 503 us; the launch traced here: 494 us
  matrix products  217 us (43%)
  blocking collectives  171 us (34%)
  local copies, waits for them, and re-layouts  61.4 us (12%)
  between operations  15.6 us (3%)
  waiting for transfers between devices  10.6 us (2%)
  starting transfers between devices  10.2 us (2%)
  other arithmetic  7.72 us (2%)
    conv_general_dilated x1, matrix products, shards(): lax.conv_general_dilated(wrapped[None], kernel, (1, 1, 1), 'VALID', dimen...  193 us
    all_gather x1, blocking collectives, shards(): gathered = lax.all_gather(x_inverse, 'gy', axis=3, tiled=True)  76.2 us
    unnamed x1, blocking collectives  57.2 us
    conv_general_dilated x5, local copies, waits for them, and re-layouts, shards(): lax.conv_general_dilated(wrapped[None], kernel, (1, 1, 1), 'VALID', dimen...  42.8 us
    all_gather x1, blocking collectives, shards(): lax.all_gather(mixed_modes, 'gx', axis=2, tiled=True)  38.1 us
  transfers between devices with their start and end apart: 5, of which 3 were waited for; matrix products, arithmetic and copies ran while one was open for 50% of the time, Pallas kernels for 0%

commit v1 on v0

--- a/solution.py
+++ b/solution.py
@@ -8,6 +8,15 @@
 KY = 24
 KZ = 12
 PRECISE = lax.Precision.HIGHEST
+
+
+def connect_the_pairs_all(view):
+    return jnp.concatenate(
+        jax.lax.all_to_all(
+            jnp.stack([view for _ in range(jax.lax.axis_size("gy"))], axis=0), "gy", 0, 0
+        ),
+        axis=3,
+    )
 
 
 def padded_2(array, sides, width):
@@ -112,7 +121,7 @@
     )
     back_real, back_imag = inverse_x(row_modes[:, 0], row_modes[:, 1], cos_x, sin_x)
     x_inverse = jnp.stack([back_real, back_imag], axis=2)
-    gathered = lax.all_gather(x_inverse, "gy", axis=3, tiled=True)
+    gathered = connect_the_pairs_all(x_inverse)
     back_real = gathered[:, :, 0].reshape(channels, cells_x, KY, KZ)
     back_imag = gathered[:, :, 1].reshape(channels, cells_x, KY, KZ)
     plane_real = jnp.einsum("cxqk,yq->cxyk", back_real, cos_y, precision=PRECISE) - jnp.einsum(

time: 503 us -> 607 us (1.21)
  the two profiles are of different devices: /device:TPU:7 before, /device:TPU:1 now
where the time goes in v1:
time: 607 us; the launch traced here: 597 us
  matrix products  237 us (39%)
  waiting for transfers between devices  130 us (21%)
  blocking collectives  94.9 us (16%)
  local copies, waits for them, and re-layouts  64.3 us (11%)
  starting transfers between devices  42.4 us (7%)
  between operations  15.5 us (3%)
  other arithmetic  13.5 us (2%)
    conv_general_dilated x1, matrix products, shards(): lax.conv_general_dilated(wrapped[None], kernel, (1, 1, 1), 'VALID', dimen...  213 us
    unnamed x2, waiting for transfers between devices  121 us
    unnamed x1, blocking collectives  62.8 us
    conv_general_dilated x5, local copies, waits for them, and re-layouts, shards(): lax.conv_general_dilated(wrapped[None], kernel, (1, 1, 1), 'VALID', dimen...  42.6 us
    all_gather x1, blocking collectives, shards(): lax.all_gather(mixed_modes, 'gx', axis=2, tiled=True)  32.1 us
    all_to_all x1, starting transfers between devices, connect_the_pairs_all(): jax.lax.all_to_all(jnp.stack([view for _ in range(jax.lax.axis_size('gy')...  27.5 us
  transfers between devices with their start and end apart: 6, of which 3 were waited for; matrix products, arithmetic and copies ran while one was open for 45% of the time, Pallas kernels for 0%

profile of v1, /device:TPU:1, one launch (start us, length us, event | category | flops | bytes accessed | tf_op | source)
XLA Modules:
  0.0 597.2 jit_solution(881018344899034786)
XLA Ops:
  6.6 2.2 convolution_bitcast_fusion
  10.1 2.1 copy.52
  14.9 1.8 fusion.13
  16.7 2.0 copy.54
  22.3 2.1 collective-permute-start
  24.4 5.4 collective-permute-start.1
  33.3 7.2 %collective-permute-start.2 = (f32[16,10,1,128]{3,0,2,1:T(8,128)S(1)}, f32[16,10,1,128]{3,0,2,1:T(8,128)S(1)}, u32[]{:S(2)}, u32[]{:S(2)}) collective-permute-start(f32[16,10,1,128]{3,0,2,1:T(8,128)S(1)} %get-tuple-element.13), channel_id=1, source_target_pairs={{0,1},{1,2},{2,3},{3,4},{4,5},{5,6},{6,7},{7,8},{8,9},{9,10},{10,1... | collective-permute-start | bytes 245768 | tf_op jit(solution)/shard_map/ppermute | solution.py:29
  42.1 7.3 %collective-permute-done.3 = f32[16,10,1,128]{3,0,2,1:T(8,128)S(1)} collective-permute-done((f32[16,10,1,128]{3,0,2,1:T(8,128)S(1)}, f32[16,10,1,128]{3,0,2,1:T(8,128)S(1)}, u32[]{:S(2)}, u32[]{:S(2)}) %collective-permute-start.3) | collective-permute-done | bytes 81952 | tf_op jit(solution)/shard_map/ppermute | solution.py:30
  51.5 6.6 %reshape.54 = f32[16,10,18,1,8,17]{5,4,0,2,1,3:T(8,128)} reshape(f32[16,10,18,1,136]{4,0,2,1,3:T(8,128)S(1)} %pad) | data formatting | bytes 3133440 | tf_op jit(solution)/shard_map/conv_general_dilated | solution.py:76
  58.0 15.0 %copy.48 = f32[16,10,18,1,8,17]{0,4,5,2,1,3:T(8,128)} copy(f32[16,10,18,1,8,17]{5,4,0,2,1,3:T(8,128)} %reshape.54) | data formatting | bytes 3133440 | tf_op jit(solution)/shard_map/conv_general_dilated | solution.py:76
  73.0 1.5 slice.80
  74.6 9.6 %fusion.198 = f32[16,10,18,8,19]{0,3,4,2,1:T(8,128)} fusion(f32[16,10,18,1,7,2]{0,4,5,2,1,3:T(8,128)S(1)} %slice.80, f32[16,10,18,1,8,17]{0,4,5,2,1,3:T(8,128)} %copy.48), kind=kLoop, calls=%fused_computation.1.clone.clone.clone.clone.1 | loop fusion | flops 1313280 | bytes 3479040 | tf_op jit(solution)/shard_map/conv_general_dilated | solution.py:76
  84.1 121.1 %all-reduce.4.cloned.1.call-done = f32[16,8,2,288]{3,1,0,2:T(8,128)} async-done(((f32[16,8,2,288]{3,1,0,2:T(8,128)}), f32[16,8,2,288]{3,1,0,2:T(8,128)}) %all-reduce.4.cloned.1.call-update) | async-done | bytes 294928
  208.1 1.4 fusion.39
  211.1 62.8 %all-reduce.1 = f32[16,2,432]{2,0,1:T(8,128)S(1)} all-reduce(f32[16,2,432]{2,0,1:T(8,128)S(1)} %pad_maximum_fusion.3), channel_id=3, replica_groups=mesh['gx'=16,'gy'=16] {'gx'}, use_global_device_ids=true, to_apply=%region_1.2.clone | all-reduce | flops 13824 | bytes 110592
  274.2 32.1 %all_gather.3 = f32[16,2,432]{0,1,2:T(2,128)S(1)} all-gather(f32[16,2,27]{0,1,2:T(2,128)S(1)} %copy.58), channel_id=1, replica_groups=mesh['gx'=16,'gy'=16] {'gx'}, dimensions={2}, use_global_device_ids=true | all-gather | bytes 58752 | tf_op jit(solution)/shard_map/all_gather | solution.py:119
  308.7 2.7 reshape.85
  311.4 27.5 %all-to-all-start = ((f32[16,1,4608]{2,1,0:T(1,128)}), f32[16,1,4608]{2,1,0:T(1,128)S(1)}, u32[]{:S(2)}, u32[]{:S(2)}) async-start(f32[16,1,4608]{2,1,0:T(1,128)} %reshape.85), calls=%async_computation | async-start | bytes 589824 | tf_op jit(solution)/shard_map/all_to_all | solution.py:15
  338.9 213.4 %broadcast_select_fusion = f32[8,16,8,17,16]{4,2,3,1,0:T(8,128)} fusion(pred[8,17]{0,1:T(8,128)(4,1)S(1)} %copy-done.7, f32[3,3,3,16,16]{4,3,2,1,0:T(8,128)S(1)} %bitcast.195, f32[16,10,18,8,19]{0,3,4,2,1:T(8,128)} %fusion.198), kind=kOutput, calls=%fused_computation.8 | convolution fusion | flops 1444167680 | bytes 2892936 | tf_op jit(solution)/shard_map/conv_general_dilated | solution.py:76
  552.4 12.5 %copy.98 = f32[8,16,8,17,16]{3,2,1,0,4:T(8,128)} copy(f32[8,16,8,17,16]{4,2,3,1,0:T(8,128)} %broadcast_select_fusion) | data formatting | bytes 2228224 | tf_op jit(solution)/shard_map/conv_general_dilated | solution.py:76
  564.9 7.0 %reshape.78 = f32[8,16,1,136,16]{3,1,0,4,2:T(8,128)} reshape(f32[8,16,8,17,16]{3,2,1,0,4:T(8,128)} %copy.98) | data formatting | bytes 2228224 | tf_op jit(solution)/shard_map/conv_general_dilated | solution.py:76
  573.7 2.4 reshape.86
  579.1 2.2 fusion.59
  585.8 4.2 fusion.19
  (85 shorter events, 29.8 us)
Async XLA Ops:
  6.5 198.7 %all-reduce.4.cloned.1.call-start = ((), (), s32[]{:S(2)}) async-start(), calls=%async_computation.1 | async-start | bytes 786432
  20.9 1.3 copy-start
  21.3 8.5 %copy-start.3 = (f32[2,16,16,1,27]{4,3,2,1,0:T(1,128)S(1)}, f32[2,16,16,1,27]{4,3,2,1,0:T(1,128)}, u32[]{:S(2)}) copy-start(f32[2,16,16,1,27]{4,3,2,1,0:T(1,128)} %param.5) | copy-start | bytes 165892
  21.3 8.5 %copy-start.6 = (u32[256]{0:T(256)S(1)}, u32[256]{0:T(256)}, u32[]{:S(2)}) copy-start(u32[256]{0:T(256)} %constant.138) | copy-start | bytes 3076
  21.4 9.1 %copy-start.5 = (u32[256]{0:T(256)S(1)}, u32[256]{0:T(256)}, u32[]{:S(2)}) copy-start(u32[256]{0:T(256)} %constant.142) | copy-start | bytes 3076
  21.4 9.8 %copy-start.4 = (f32[27,16,16]{0,2,1:T(8,128)S(1)}, f32[27,16,16]{0,2,1:T(8,128)}, u32[]{:S(2)}) copy-start(f32[27,16,16]{0,2,1:T(8,128)} %param.4) | copy-start | bytes 82948
  22.3 10.4 %collective-permute-start = (f32[16,1,16,128]{3,0,2,1:T(8,128)S(1)}, f32[16,1,16,128]{3,0,2,1:T(8,128)S(1)}, u32[]{:S(2)}, u32[]{:S(2)}) collective-permute-start(f32[16,1,16,128]{3,0,2,1:T(8,128)S(1)} %copy.110), channel_id=1, source_target_pairs={{0,16},{16,32},{32,48},{48,64},{64,80},{80,96},{96,112},{112,128},... | collective-permute-start | bytes 393224 | tf_op jit(solution)/shard_map/ppermute | solution.py:29
  24.4 8.9 %collective-permute-start.1 = (f32[16,1,16,128]{3,0,2,1:T(8,128)S(1)}, f32[16,1,16,128]{3,0,2,1:T(8,128)S(1)}, u32[]{:S(2)}, u32[]{:S(2)}) collective-permute-start(f32[16,1,16,128]{3,0,2,1:T(8,128)S(1)} %copy.111), channel_id=1, source_target_pairs={{16,0},{32,16},{48,32},{64,48},{80,64},{96,80},{112,96},{128,112},... | collective-permute-start | bytes 393224 | tf_op jit(solution)/shard_map/ppermute | solution.py:30
  33.3 8.7 %collective-permute-start.2 = (f32[16,10,1,128]{3,0,2,1:T(8,128)S(1)}, f32[16,10,1,128]{3,0,2,1:T(8,128)S(1)}, u32[]{:S(2)}, u32[]{:S(2)}) collective-permute-start(f32[16,10,1,128]{3,0,2,1:T(8,128)S(1)} %get-tuple-element.13), channel_id=1, source_target_pairs={{0,1},{1,2},{2,3},{3,4},{4,5},{5,6},{6,7},{7,8},{8,9},{9,10},{10,1... | collective-permute-start | bytes 245768 | tf_op jit(solution)/shard_map/ppermute | solution.py:29
  40.5 8.8 %collective-permute-start.3 = (f32[16,10,1,128]{3,0,2,1:T(8,128)S(1)}, f32[16,10,1,128]{3,0,2,1:T(8,128)S(1)}, u32[]{:S(2)}, u32[]{:S(2)}) collective-permute-start(f32[16,10,1,128]{3,0,2,1:T(8,128)S(1)} %get-tuple-element.14), channel_id=1, source_target_pairs={{1,0},{2,1},{3,2},{4,3},{5,4},{6,5},{7,6},{8,7},{9,8},{10,9},{11,1... | collective-permute-start | bytes 245768 | tf_op jit(solution)/shard_map/ppermute | solution.py:30
  308.7 30.2 %copy-start.7 = (pred[8,17]{0,1:T(8,128)(4,1)S(1)}, pred[8,17]{0,1:T(8,128)(4,1)}, u32[]{:S(2)}) copy-start(pred[8,17]{0,1:T(8,128)(4,1)} %constant.131) | copy-start | bytes 412
  311.4 260.4 %all-to-all-start = ((f32[16,1,4608]{2,1,0:T(1,128)}), f32[16,1,4608]{2,1,0:T(1,128)S(1)}, u32[]{:S(2)}, u32[]{:S(2)}) async-start(f32[16,1,4608]{2,1,0:T(1,128)} %reshape.85), calls=%async_computation | async-start | bytes 589824 | tf_op jit(solution)/shard_map/all_to_all | solution.py:15
  581.8 1.2 copy-start.1
  584.2 1.6 copy-start.2
Sparse Core Ops, SparseCore 0:
  22.3 182.8 all-reduce.3
